TPU v7x, 32 devices: a whole 2x2x4 slice. The times are simulated.
32 devices in a mesh: member: 2 (over y), polar: 4 (over z), azimuth: 4 (over x, core).
Axes of the slice: x: 2, y: 2, z: 4, core: 2. Of those that a mesh axis runs over, the one named last changes fastest.
Arguments:
- conv_out: bfloat16 [32, 720, 640], P(('member', 'polar'), 'azimuth'), parts along dimension 0, may hold values from -6 to 6
- grad_out: bfloat16 [32, 720, 640], P(('member', 'polar'), 'azimuth'), parts along dimension 0, may hold values from -6 to 6
- w_in: bfloat16 [640, 1280], replicated, may hold values from -0.25 to 0.25
- b_in: float32 [1280], replicated, may hold values from -4 to 4
- w_out: bfloat16 [1280, 640], replicated, may hold values from -0.15625 to 0.15625
- basis_weight: float32 [9, 640], replicated, may hold values from -1 to 1
- filt: bfloat16 [9, 16, 640], replicated, may hold values from -2 to 2
- offsets: int32 [16, 9], replicated, may hold values from 0 to 15, as said below
Outputs:
- grad_in: bfloat16 [32, 720, 640], P(('member', 'polar'), 'azimuth'), parts along dimension 0
There are 2 independent parts, one for each index of `member`. A program takes and returns all parts, laid end to end along the dimension named above; an argument that names none is the same for every part. Nothing has to cross between parts.
Inputs may be any that keep to these rules, and one draw needn't show every extreme that they name: offsets[i, k] lies within 3 rows of i; column 0 is i, column 1 is min(i + 3, 15), column 2 is max(i - 3, 0).
All inputs are finite; a program needn't handle non-finite values.
Results may differ from a plain program's by a relative error of at most 0.006.
Values may be sent and summed in bfloat16 or wider, within the bound.
A program may use at most 64 MiB of HBM per device.

v0:
```python
import functools
import math

import jax
import jax.numpy as jnp
import ml_dtypes
import numpy as np
from jax import lax
from jax.experimental import pallas as pl
from jax.experimental.pallas import tpu as pltpu
from jax.sharding import PartitionSpec as P

REACH = 3
LANES = 128
MESH = pl.DeviceIdType.MESH
F32 = jnp.float32
BF16 = jnp.bfloat16


def fourier_tables(length, modes):
    phase = np.arange(length)[:, None] * np.arange(modes)[None, :] % length
    angle = 2.0 * math.pi / length * phase
    scale = 1.0 / math.sqrt(length)
    factor = np.where(np.arange(modes) == 0, 1.0, 2.0)[None, :]
    analysis = np.concatenate([np.cos(angle), -np.sin(angle)], axis=1) * scale
    synth = np.concatenate([np.cos(angle) * factor, -np.sin(angle) * factor], axis=1) * scale
    return analysis, synth


def gelu_slope(values):
    normal_cdf = 0.5 * (1.0 + lax.erf(values * (1.0 / math.sqrt(2.0))))
    density = jnp.exp(-0.5 * values * values) * (1.0 / math.sqrt(2.0 * math.pi))
    return normal_cdf + values * density


def dot(a, b):
    return jnp.dot(a, b, preferred_element_type=F32)


def dot_nt(a, b):
    return lax.dot_general(a, b, (((1,), (1,)), ((), ())), preferred_element_type=F32)


def dot_tn(a, b):
    return lax.dot_general(a, b, (((0,), (0,)), ((), ())), preferred_element_type=F32)


def kernel(
    parts, bands, conv, grad, w_in, b_in, w_out, wexp, target, fsel, ana, syn,
    out,
    w_perm, slope, tails, send, recv, spec, spec_tail, gain, outspec, ret_send, ret_recv,
    a_send, a_recv, z_send, z_recv, r_send, r_recv,
):
    rows, lon, channels = conv.shape
    hidden = w_in.shape[1]
    chan_part = channels // parts
    tail = chan_part - LANES
    me = lax.axis_index("azimuth")
    band = lax.axis_index("polar")
    bases2 = wexp.shape[0]
    width = rows + 2 * REACH
    modes2 = ana.shape[1]
    modes = modes2 // 2
    has_low = band > 0
    has_high = band < bands - 1

    barrier = pltpu.get_barrier_semaphore()
    for step in range(1, parts):
        pl.semaphore_signal(
            barrier, inc=1, device_id={"azimuth": lax.rem(me + step, parts)}, device_id_type=MESH
        )

    @pl.when(has_low)
    def _():
        pl.semaphore_signal(barrier, inc=1, device_id={"polar": band - 1}, device_id_type=MESH)

    @pl.when(has_high)
    def _():
        pl.semaphore_signal(barrier, inc=1, device_id={"polar": band + 1}, device_id_type=MESH)

    for part in range(parts):
        w_perm[part * LANES : (part + 1) * LANES, :] = w_in[
            part * chan_part : part * chan_part + LANES, :
        ]
        w_perm[parts * LANES + part * tail : parts * LANES + (part + 1) * tail, :] = w_in[
            part * chan_part + LANES : (part + 1) * chan_part, :
        ]

    neighbours = jnp.where(has_low, 1, 0) + jnp.where(has_high, 1, 0)
    pl.semaphore_wait(barrier, parts - 1 + neighbours)

    def out_copy(step, tile):
        peer = lax.rem(me + step, parts)
        return pltpu.make_async_remote_copy(
            src_ref=send.at[peer, tile], dst_ref=recv.at[tile, me],
            send_sem=a_send.at[step, tile], recv_sem=a_recv.at[step, tile],
            device_id={"azimuth": peer}, device_id_type=MESH,
        )

    def in_copy(step, tile):
        peer = lax.rem(me + parts - step, parts)
        return pltpu.make_async_remote_copy(
            src_ref=send.at[peer, tile], dst_ref=recv.at[tile, peer],
            send_sem=a_send.at[step, tile], recv_sem=a_recv.at[step, tile],
            device_id={"azimuth": peer}, device_id_type=MESH,
        )

    def row_order(it):
        return lax.rem(it * (rows - 1), rows)

    piece = 2 * LANES

    def mlp_row(it, carry):
        row = row_order(it)
        for at in range(0, hidden, piece):
            pre = dot(conv[row], w_in[:, at : at + piece]) + b_in[:, at : at + piece]
            back = dot_nt(grad[row], w_out[at : at + piece, :])
            slope[:, at : at + piece] = (back * gelu_slope(pre)).astype(BF16)
        full = dot_nt(slope[...], w_perm[...]).astype(BF16)
        for part in range(parts):
            send[part, row] = full[:, part * LANES : (part + 1) * LANES]
        tails[row] = full[:, parts * LANES :]
        recv[row, me] = send[me, row]
        for step in range(1, parts):
            out_copy(step, row).start()
        return carry

    lax.fori_loop(0, rows, mlp_row, 0)
    for part in range(parts):
        send[part, rows] = jnp.concatenate(
            [tails[row][:, part * tail : (part + 1) * tail] for row in range(rows)], axis=1
        )
    recv[rows, me] = send[me, rows]
    for step in range(1, parts):
        out_copy(step, rows).start()

    index = lax.broadcasted_iota(jnp.int32, (bases2, LANES), 0)
    half = bases2 // 2
    index = jnp.where(index >= half, index - half, index)
    source = lax.rem(index, width)
    lane_row = lax.broadcasted_iota(jnp.int32, (bases2, LANES), 1) // tail
    weights = wexp[...]
    top = weights.astype(BF16).astype(F32)
    first = lax.broadcasted_iota(jnp.int32, weights.shape, 0) < half
    weights = jnp.where(first, top, weights - top)
    w_main = weights[:, :LANES]
    w_tail = weights[:, LANES:]
    goal = target[...]
    f_t = fsel[...]

    reach2 = 2 * REACH + 1

    def pair_gain(idx, carry):
        j = idx // reach2
        shift = lax.rem(idx, reach2)
        keep = (goal == j) & (source == j + shift)
        gain[idx] = dot_tn(f_t, jnp.where(keep, w_main, 0.0).astype(BF16))
        return carry

    lax.fori_loop(0, rows * reach2, pair_gain, 0)

    def tail_gain(shift, carry):
        keep = (goal == lane_row) & (source == lane_row + shift)
        gain[rows * reach2 + shift] = dot_tn(f_t, jnp.where(keep, w_tail, 0.0).astype(BF16))
        return carry

    lax.fori_loop(0, reach2, tail_gain, 0)

    @pl.when(jnp.logical_not(has_low))
    def _():
        spec[0:REACH] = jnp.zeros((REACH, modes2, LANES), BF16)
        spec_tail[0] = jnp.zeros((modes2, LANES), BF16)

    @pl.when(jnp.logical_not(has_high))
    def _():
        spec[REACH + rows :] = jnp.zeros((REACH, modes2, LANES), BF16)
        spec_tail[2] = jnp.zeros((modes2, LANES), BF16)

    def up_copy(row):
        if row == rows:
            src, dst = spec_tail.at[1], spec_tail.at[0]
        else:
            src, dst = spec.at[REACH + row], spec.at[REACH + row - rows]
        return pltpu.make_async_remote_copy(
            src_ref=src, dst_ref=dst, send_sem=z_send.at[0, row], recv_sem=z_recv.at[0, row],
            device_id={"polar": band + 1}, device_id_type=MESH,
        )

    def down_copy(row):
        if row == rows:
            src, dst = spec_tail.at[1], spec_tail.at[2]
        else:
            src, dst = spec.at[REACH + row], spec.at[REACH + row + rows]
        return pltpu.make_async_remote_copy(
            src_ref=src, dst_ref=dst, send_sem=z_send.at[1, row], recv_sem=z_recv.at[1, row],
            device_id={"polar": band - 1}, device_id_type=MESH,
        )

    def start_up(row):
        @pl.when(has_high)
        def _():
            up_copy(row).start()

    def start_down(row):
        @pl.when(has_low)
        def _():
            down_copy(row).start()

    def analyze(tile):
        for step in range(1, parts):
            in_copy(step, tile).wait_recv()
        total = dot(ana[0], recv[tile, 0])
        for src in range(1, parts):
            total = total + dot(ana[src], recv[tile, src])
        return total.astype(BF16)

    later = []
    for it in range(rows):
        row = it * (rows - 1) % rows
        spec[REACH + row] = analyze(row)
        if row >= rows - REACH:
            if row >= rows - REACH + 1:
                start_up(row)
            else:
                later.append((start_up, row))
        if row < REACH:
            if row < REACH - 1:
                start_down(row)
            else:
                later.append((start_down, row))
    for start, row in later:
        start(row)
    spec_tail[1] = analyze(rows)
    start_up(rows)
    start_down(rows)

    def back_copy(step, tile):
        peer = lax.rem(me + step, parts)
        return pltpu.make_async_remote_copy(
            src_ref=ret_send.at[peer, tile], dst_ref=ret_recv.at[me, tile],
            send_sem=r_send.at[step, tile], recv_sem=r_recv.at[step, tile],
            device_id={"azimuth": peer}, device_id_type=MESH,
        )

    def back_in(step, tile):
        peer = lax.rem(me + parts - step, parts)
        return pltpu.make_async_remote_copy(
            src_ref=ret_send.at[peer, tile], dst_ref=ret_recv.at[peer, tile],
            send_sem=r_send.at[step, tile], recv_sem=r_recv.at[step, tile],
            device_id={"azimuth": peer}, device_id_type=MESH,
        )

    chunk = 64

    def finish(tile):
        values = outspec[...]
        for part in range(parts):
            ret_send[part, tile] = dot(syn[part], values).astype(BF16)
        ret_recv[me, tile] = ret_send[me, tile]
        for step in range(1, parts):
            back_copy(step, tile).start()

    def filter_main(j):
        def one(it, carry):
            lo = pl.ds(it * chunk, chunk)
            hi = pl.ds(modes + it * chunk, chunk)
            real = jnp.zeros((chunk, LANES), F32)
            imag = jnp.zeros((chunk, LANES), F32)
            for shift in range(reach2):
                gr, gi = gain[j * reach2 + shift, lo, :], gain[j * reach2 + shift, hi, :]
                sr = spec[j + shift, lo, :].astype(F32)
                si = spec[j + shift, hi, :].astype(F32)
                real = real + gr * sr + gi * si
                imag = imag + gr * si - gi * sr
            outspec[lo, :] = real.astype(BF16)
            outspec[hi, :] = imag.astype(BF16)
            return carry

        lax.fori_loop(0, modes // chunk, one, 0)

    def window(ref, at, shift):
        low, own, high = (ref[k, at, :].astype(F32) for k in range(3))
        result = []
        lane = lax.broadcasted_iota(jnp.int32, own.shape, 1)
        delta = (shift - REACH) * tail
        if delta == 0:
            return own
        if delta < 0:
            turn = -delta
            return jnp.where(lane < turn, pltpu.roll(low, turn, 1), pltpu.roll(own, turn, 1))
        turn = LANES - delta
        return jnp.where(lane < turn, pltpu.roll(own, turn, 1), pltpu.roll(high, turn, 1))

    def filter_tail():
        def one(it, carry):
            lo = pl.ds(it * chunk, chunk)
            hi = pl.ds(modes + it * chunk, chunk)
            real = jnp.zeros((chunk, LANES), F32)
            imag = jnp.zeros((chunk, LANES), F32)
            for shift in range(reach2):
                at = rows * reach2 + shift
                gr, gi = gain[at, lo, :], gain[at, hi, :]
                sr, si = window(spec_tail, lo, shift), window(spec_tail, hi, shift)
                real = real + gr * sr + gi * si
                imag = imag + gr * si - gi * sr
            outspec[lo, :] = real.astype(BF16)
            outspec[hi, :] = imag.astype(BF16)
            return carry

        lax.fori_loop(0, modes // chunk, one, 0)

    low_left = list(range(rows - REACH, rows))
    high_left = list(range(REACH))

    def wait_low(row):
        if row in low_left:
            low_left.remove(row)

            @pl.when(has_low)
            def _():
                up_copy(row).wait_recv()

    def wait_high(row):
        if row in high_left:
            high_left.remove(row)

            @pl.when(has_high)
            def _():
                down_copy(row).wait_recv()

    for j in sorted(range(rows), key=lambda j: max(REACH - j, j + REACH - rows + 1)):
        for row in range(j - REACH, 0):
            wait_low(row + rows)
        for row in range(rows, j + REACH + 1):
            wait_high(row - rows)
        filter_main(j)
        finish(j)

    @pl.when(has_low)
    def _():
        up_copy(rows).wait_recv()

    @pl.when(has_high)
    def _():
        down_copy(rows).wait_recv()

    filter_tail()
    finish(rows)

    for tile in range(rows + 1):
        for step in range(1, parts):
            out_copy(step, tile).wait_send()
    for row in list(range(rows - REACH, rows)) + [rows]:

        @pl.when(has_high)
        def _():
            up_copy(row).wait_send()

    for row in list(range(REACH)) + [rows]:

        @pl.when(has_low)
        def _():
            down_copy(row).wait_send()

    for tile in range(rows + 1):
        for step in range(1, parts):
            back_in(step, tile).wait_recv()
    for row in range(rows):
        pieces = []
        for src in range(parts):
            pieces.append(ret_recv[src, row])
            pieces.append(ret_recv[src, rows][:, row * tail : (row + 1) * tail])
        out[row] = jnp.concatenate(pieces, axis=1)
    for tile in range(rows + 1):
        for step in range(1, parts):
            back_copy(step, tile).wait_send()


def on_device(parts, bands, conv_out, grad_out, w_in, b_in, w_out, basis_weight, filt, offsets):
    rows, lon, channels = conv_out.shape
    hidden = w_in.shape[1]
    chan_part = channels // parts
    tail = chan_part - LANES
    assert 0 < tail and rows * tail == LANES and rows >= REACH
    modes2 = filt.shape[2]
    modes = modes2 // 2
    bases = filt.shape[0]
    width = rows + 2 * REACH
    analysis, synth = fourier_tables(parts * lon, modes)
    ana = np.ascontiguousarray(
        analysis.reshape(parts, lon, modes2).transpose(0, 2, 1)
    ).astype(ml_dtypes.bfloat16)
    syn = synth.reshape(parts, lon, modes2).astype(ml_dtypes.bfloat16)
    start_lat = lax.axis_index("polar") * rows
    start_chan = lax.axis_index("azimuth") * chan_part
    pad = ((0, 0), (REACH, REACH), (0, 0))
    fsel = lax.dynamic_slice_in_dim(jnp.pad(filt, pad), start_lat, width, 1)
    fsel = fsel.reshape(bases * width, modes2)
    fsel = jnp.concatenate([fsel, fsel], axis=0)
    goal = lax.dynamic_slice_in_dim(jnp.pad(offsets.T, pad[:2]), start_lat, width, 1) - start_lat
    goal = goal.reshape(bases * width)
    goal = jnp.broadcast_to(jnp.concatenate([goal, goal])[:, None], (2 * bases * width, LANES))
    weights = lax.dynamic_slice_in_dim(basis_weight, start_chan, chan_part, 1)
    wexp = jnp.concatenate([weights[:, :LANES]] + [weights[:, LANES:]] * rows, axis=1)
    wexp = jnp.broadcast_to(wexp[None, :, None, :], (2, bases, width, 2 * LANES))
    wexp = wexp.reshape(2 * bases * width, 2 * LANES)
    tiles = rows + 1
    vmem = pl.BlockSpec(memory_space=pltpu.VMEM)
    dma = pltpu.SemaphoreType.DMA
    reach2 = 2 * REACH + 1
    returned = pl.pallas_call(
        functools.partial(kernel, parts, bands),
        out_shape=jax.ShapeDtypeStruct((rows, lon, channels), BF16),
        in_specs=[vmem] * 10,
        out_specs=vmem,
        scratch_shapes=[
            pltpu.VMEM((channels, hidden), BF16),
            pltpu.VMEM((lon, hidden), BF16),
            pltpu.VMEM((rows, lon, parts * tail), BF16),
            pltpu.VMEM((parts, tiles, lon, LANES), BF16),
            pltpu.VMEM((tiles, parts, lon, LANES), BF16),
            pltpu.VMEM((width, modes2, LANES), BF16),
            pltpu.VMEM((3, modes2, LANES), BF16),
            pltpu.VMEM((tiles * reach2, modes2, LANES), F32),
            pltpu.VMEM((modes2, LANES), BF16),
            pltpu.VMEM((parts, tiles, lon, LANES), BF16),
            pltpu.VMEM((parts, tiles, lon, LANES), BF16),
            dma((parts, tiles)),
            dma((parts, tiles)),
            dma((2, tiles)),
            dma((2, tiles)),
            dma((parts, tiles)),
            dma((parts, tiles)),
        ],
        compiler_params=pltpu.CompilerParams(
            collective_id=0, has_side_effects=True, vmem_limit_bytes=56 * 1024 * 1024
        ),
    )(conv_out, grad_out, w_in, b_in[None, :], w_out, wexp, goal, fsel, jnp.asarray(ana),
      jnp.asarray(syn))
    return (grad_out.astype(F32) + returned.astype(F32)).astype(BF16)


def solution(mesh):
    grid = P(("member", "polar"), "azimuth", None)
    return jax.shard_map(
        functools.partial(on_device, mesh.shape["azimuth"], mesh.shape["polar"]),
        mesh=mesh,
        in_specs=(grid, grid, P(), P(), P(), P(), P(), P()),
        out_specs=grid,
        check_vma=False,
    )
```

profile of v0, /device:TPU:1, one launch (start us, length us, event | category | flops | bytes accessed | tf_op | source)
XLA Modules:
  0.0 58.4 jit_solution(15105337635093645680)
XLA Ops:
  0.0 0.0 copy-start
  0.0 0.0 copy-start.2
  0.0 1.4 %broadcast_in_dim.6.b_in = f32[1,1280]{1,0:T(1,128)} reshape(f32[1280]{0:T(1024)} %param.13) | data formatting | bytes 10240 | tf_op jit(solution)/shard_map/broadcast_in_dim | solution.py:438
  1.4 0.7 %fusion = s32[9,10]{0,1:T(8,128)S(1)} fusion(s32[]{:T(128)S(6)} %select_n.8, s32[9,16]{0,1:T(8,128)} %bitcast.1, s32[]{:T(128)S(6)} %mul.7), kind=kLoop, calls=%fused_computation.5 | loop fusion | flops 90 | bytes 944 | tf_op jit(solution)/shard_map/sub | solution.py:400
  2.1 0.1 copy.17
  2.2 0.1 reshape.12
  2.3 0.1 pad_add_fusion
  2.3 0.0 copy-done
  2.3 0.1 constant_dynamic-slice_fusion
  2.4 0.1 constant_dynamic-slice_fusion.1
  2.5 0.1 pad_maximum_fusion.1
  2.6 0.7 %broadcast_in_dim.8.target = s32[180,128]{1,0:T(8,128)} broadcast(s32[180]{0:T(256)S(1)} %pad_add_fusion), dimensions={0} | broadcast | bytes 92880 | tf_op jit(solution)/shard_map/broadcast_in_dim | solution.py:402
  3.3 1.0 %pad_dynamic-slice_fusion = bf16[9,10,640]{2,1,0:T(8,128)(2,1)S(1)} fusion(s32[]{:T(128)S(6)} %select_n.8, bf16[9,16,640]{2,1,0:T(8,128)(2,1)} %param.16), kind=kLoop, calls=%fused_computation.1 | loop fusion | bytes 299524 | tf_op jit(solution)/shard_map/dynamic_slice | solution.py:397
  4.3 0.0 copy-start.1
  4.4 0.7 %pad_maximum_fusion.fsel = bf16[180,640]{1,0:T(8,128)(2,1)} fusion(bf16[90,640]{1,0:T(8,128)(2,1)S(1)} %reshape.13), kind=kLoop, calls=%fused_computation.2 | loop fusion | flops 460800 | bytes 345600 | tf_op jit(solution)/shard_map/concatenate | solution.py:399
  5.1 0.7 %reshape.11.wexp = f32[180,256]{1,0:T(8,128)} reshape(f32[2,9,10,256]{3,2,1,0:T(8,128)S(1)} %broadcast_in_dim.7) | data formatting | bytes 368640 | tf_op jit(solution)/shard_map/reshape | solution.py:406
  5.8 0.0 copy-done.2
  5.8 1.0 %copy.18.conv = bf16[4,180,640]{2,1,0:T(8,128)(2,1)} copy(bf16[4,180,640]{2,0,1:T(4,128)(2,1)S(1)} %copy-done.2) | data formatting | bytes 1843200 | tf_op args[0]
  6.9 0.0 copy-done.1
  6.9 1.1 %copy.16.grad = bf16[4,180,640]{2,1,0:T(8,128)(2,1)} copy(bf16[4,180,640]{2,0,1:T(4,128)(2,1)S(1)} %copy-done.1) | data formatting | bytes 1843200 | tf_op args[1]
  8.0 47.8 %shard_map.100 = bf16[4,180,640]{2,1,0:T(8,128)(2,1)} custom-call(bf16[4,180,640]{2,1,0:T(8,128)(2,1)} %copy.18.conv, bf16[4,180,640]{2,1,0:T(8,128)(2,1)} %copy.16.grad, bf16[640,1280]{1,0:T(8,128)(2,1)} %w_in.1, f32[1,1280]{1,0:T(1,128)} %broadcast_in_dim.6.b_in, bf16[1280,640]{1,0:T(8,128)(2,1)} %w_out.1, f32[180,256]{1,0:T(8,128)} %reshape.11.wexp, ...), custom_call_target="tpu_custom_call" | custom-call | tf_op jit(solution)/shard_map/pallas_call | solution.py:411
  55.7 1.4 %add_convert_fusion = bf16[4,180,640]{2,1,0:T(8,128)(2,1)S(1)} fusion(bf16[4,180,640]{2,1,0:T(8,128)(2,1)} %shard_map.100, bf16[4,180,640]{2,0,1:T(4,128)(2,1)S(1)} %copy-done.1), kind=kLoop, calls=%fused_computation | loop fusion | flops 1843200 | bytes 2764800 | tf_op jit(solution)/shard_map/convert_element_type | solution.py:440
  57.1 1.3 %copy.20 = bf16[4,180,640]{2,0,1:T(4,128)(2,1)} copy(bf16[4,180,640]{2,1,0:T(8,128)(2,1)S(1)} %add_convert_fusion) | data formatting | bytes 1843200 | tf_op jit(solution)/shard_map/convert_element_type | solution.py:440
  (2 shorter events, 0.1 us)
Async XLA Ops:
  0.0 2.3 %copy-start = (f32[9,640]{1,0:T(8,128)S(1)}, f32[9,640]{1,0:T(8,128)}, u32[]{:S(2)}) copy-start(f32[9,640]{1,0:T(8,128)} %param.15) | copy-start | bytes 69124
  0.0 5.8 %copy-start.2 = (bf16[4,180,640]{2,0,1:T(4,128)(2,1)S(1)}, bf16[4,180,640]{2,0,1:T(4,128)(2,1)}, u32[]{:S(2)}) copy-start(bf16[4,180,640]{2,0,1:T(4,128)(2,1)} %param.10) | copy-start | bytes 2764804
  4.3 2.6 %copy-start.1 = (bf16[4,180,640]{2,0,1:T(4,128)(2,1)S(1)}, bf16[4,180,640]{2,0,1:T(4,128)(2,1)}, u32[]{:S(2)}) copy-start(bf16[4,180,640]{2,0,1:T(4,128)(2,1)} %param.11) | copy-start | bytes 2764804
where the time goes:
time: 58.8 us; the launch traced here: 58.4 us
  Pallas kernels  47.8 us (81%)
  local copies, waits for them, and re-layouts  7.61 us (13%)
  other arithmetic  2.96 us (5%)
    pallas_call x1, Pallas kernels, on_device(): pl.pallas_call(functools.partial(kernel, parts, bands), out_shape=jax.Sha...  47.8 us
    unnamed x8, local copies, waits for them, and re-layouts  2.13 us
    broadcast_in_dim x1, local copies, waits for them, and re-layouts, on_device(): b_in[None, :]  1.37 us
    convert_element_type x1, other arithmetic, on_device(): return (grad_out.astype(F32) + returned.astype(F32)).astype(BF16)  1.37 us
    convert_element_type x1, local copies, waits for them, and re-layouts, on_device(): return (grad_out.astype(F32) + returned.astype(F32)).astype(BF16)  1.28 us

commit v1 on v0

--- a/solution.py
+++ b/solution.py
@@ -46,9 +46,9 @@
 
 
 def kernel(
-    parts, bands, conv, grad, w_in, b_in, w_out, wexp, target, fsel, ana, syn,
+    parts, bands, conv, grad, w_in, b_in, w_out, weight, filt, offsets, ana, syn,
     out,
-    w_perm, slope, tails, send, recv, spec, spec_tail, gain, outspec, ret_send, ret_recv,
+    w_perm, slope, tails, send, recv, spec, spec_tail, gain, flipped, outspec, ret_send, ret_recv,
     a_send, a_recv, z_send, z_recv, r_send, r_recv,
 ):
     rows, lon, channels = conv.shape
@@ -57,10 +57,10 @@
     tail = chan_part - LANES
     me = lax.axis_index("azimuth")
     band = lax.axis_index("polar")
-    bases2 = wexp.shape[0]
+    bases, lat, modes2 = filt.shape
     width = rows + 2 * REACH
-    modes2 = ana.shape[1]
     modes = modes2 // 2
+    reach2 = 2 * REACH + 1
     has_low = band > 0
     has_high = band < bands - 1
 
@@ -113,7 +113,7 @@
     def mlp_row(it, carry):
         row = row_order(it)
         for at in range(0, hidden, piece):
-            pre = dot(conv[row], w_in[:, at : at + piece]) + b_in[:, at : at + piece]
+            pre = dot(conv[row], w_in[:, at : at + piece]) + b_in[at : at + piece][None, :]
             back = dot_nt(grad[row], w_out[at : at + piece, :])
             slope[:, at : at + piece] = (back * gelu_slope(pre)).astype(BF16)
         full = dot_nt(slope[...], w_perm[...]).astype(BF16)
@@ -134,38 +134,6 @@
     for step in range(1, parts):
         out_copy(step, rows).start()
 
-    index = lax.broadcasted_iota(jnp.int32, (bases2, LANES), 0)
-    half = bases2 // 2
-    index = jnp.where(index >= half, index - half, index)
-    source = lax.rem(index, width)
-    lane_row = lax.broadcasted_iota(jnp.int32, (bases2, LANES), 1) // tail
-    weights = wexp[...]
-    top = weights.astype(BF16).astype(F32)
-    first = lax.broadcasted_iota(jnp.int32, weights.shape, 0) < half
-    weights = jnp.where(first, top, weights - top)
-    w_main = weights[:, :LANES]
-    w_tail = weights[:, LANES:]
-    goal = target[...]
-    f_t = fsel[...]
-
-    reach2 = 2 * REACH + 1
-
-    def pair_gain(idx, carry):
-        j = idx // reach2
-        shift = lax.rem(idx, reach2)
-        keep = (goal == j) & (source == j + shift)
-        gain[idx] = dot_tn(f_t, jnp.where(keep, w_main, 0.0).astype(BF16))
-        return carry
-
-    lax.fori_loop(0, rows * reach2, pair_gain, 0)
-
-    def tail_gain(shift, carry):
-        keep = (goal == lane_row) & (source == lane_row + shift)
-        gain[rows * reach2 + shift] = dot_tn(f_t, jnp.where(keep, w_tail, 0.0).astype(BF16))
-        return carry
-
-    lax.fori_loop(0, reach2, tail_gain, 0)
-
     @pl.when(jnp.logical_not(has_low))
     def _():
         spec[0:REACH] = jnp.zeros((REACH, modes2, LANES), BF16)
@@ -214,25 +182,78 @@
             total = total + dot(ana[src], recv[tile, src])
         return total.astype(BF16)
 
-    later = []
-    for it in range(rows):
-        row = it * (rows - 1) % rows
+    order = [it * (rows - 1) % rows for it in range(rows)]
+    done = []
+    ups = list(range(rows - 1, rows - REACH, -1))
+    downs = list(range(REACH - 1))
+    for row in order:
         spec[REACH + row] = analyze(row)
-        if row >= rows - REACH:
-            if row >= rows - REACH + 1:
-                start_up(row)
-            else:
-                later.append((start_up, row))
-        if row < REACH:
-            if row < REACH - 1:
-                start_down(row)
-            else:
-                later.append((start_down, row))
-    for start, row in later:
-        start(row)
+        done.append(row)
+        while ups and ups[0] in done:
+            start_up(ups.pop(0))
+        while downs and downs[0] in done:
+            start_down(downs.pop(0))
     spec_tail[1] = analyze(rows)
     start_up(rows)
     start_down(rows)
+    start_up(rows - REACH)
+    start_down(REACH - 1)
+
+    half = bases * width
+    lines = 2 * half
+
+    def line_parts(lanes):
+        line = lax.broadcasted_iota(jnp.int32, (lines, lanes), 0)
+        low_bits = line >= half
+        line = jnp.where(low_bits, line - half, line)
+        basis = line // width
+        return low_bits, basis, line - basis * width, lax.broadcasted_iota(jnp.int32, (lines, lanes), 1)
+
+    start_lat = band * rows - REACH
+    low_bits, basis, place, lane = line_parts(bases * lat)
+    pick = jnp.where(lane == basis * lat + place + start_lat, 1.0, 0.0)
+    pick = jnp.where((place + start_lat >= 0) & (place + start_lat < lat), pick, 0.0)
+    f_t = dot(pick.astype(BF16), filt[...].reshape(bases * lat, modes2))
+    low_bits, basis, place, lane = line_parts(lat)
+    pick = jnp.where(lane == place + start_lat, 1.0, 0.0).astype(BF16)
+    rows_of = dot(pick, offsets[...].astype(F32).astype(BF16))
+    low_bits, basis, place, lane = line_parts(bases)
+    goal = jnp.sum(jnp.where(lane == basis, rows_of, 0.0), axis=1, keepdims=True)
+    goal = jnp.broadcast_to(goal.astype(jnp.int32) - band * rows, (lines, LANES))
+    weights = weight[:, :chan_part]
+    for part in range(1, parts):
+        mine = weight[:, part * chan_part : (part + 1) * chan_part]
+        weights = jnp.where(me == part, mine, weights)
+    top = weights.astype(BF16)
+    rest = (weights - top.astype(F32)).astype(BF16)
+    chosen = jnp.where(lane == basis, 1.0, 0.0)
+    weights = dot(jnp.where(low_bits, 0.0, chosen).astype(BF16), top) + dot(
+        jnp.where(low_bits, chosen, 0.0).astype(BF16), rest
+    )
+    w_main = weights[:, :LANES]
+    w_tail = jnp.concatenate([weights[:, LANES:]] * rows, axis=1)
+    low_bits, basis, source, lane = line_parts(LANES)
+    lane_row = lane // tail
+
+    flipped[...] = jnp.transpose(f_t).astype(BF16)
+
+    def tile_gain(tile, carry):
+        goal_row = jnp.where(tile == rows, lane_row, tile)
+        scale = jnp.where(tile == rows, w_tail, w_main)
+        aimed = jnp.where(goal == goal_row, scale, 0.0)
+        table = jnp.concatenate(
+            [
+                jnp.where(source == goal_row + shift, aimed, 0.0).astype(BF16)
+                for shift in range(reach2)
+            ],
+            axis=1,
+        )
+        made = dot(flipped[...], table)
+        for shift in range(reach2):
+            gain[tile * reach2 + shift] = made[:, shift * LANES : (shift + 1) * LANES]
+        return carry
+
+    lax.fori_loop(0, rows + 1, tile_gain, 0)
 
     def back_copy(step, tile):
         peer = lax.rem(me + step, parts)
@@ -328,7 +349,10 @@
             def _():
                 down_copy(row).wait_recv()
 
-    for j in sorted(range(rows), key=lambda j: max(REACH - j, j + REACH - rows + 1)):
+    def need_all(j):
+        return j - REACH <= -REACH or j + REACH >= rows + REACH - 1
+
+    def finish_row(j):
         for row in range(j - REACH, 0):
             wait_low(row + rows)
         for row in range(rows, j + REACH + 1):
@@ -336,6 +360,10 @@
         filter_main(j)
         finish(j)
 
+    for j in range(rows):
+        if not need_all(j):
+            finish_row(j)
+
     @pl.when(has_low)
     def _():
         up_copy(rows).wait_recv()
@@ -346,6 +374,9 @@
 
     filter_tail()
     finish(rows)
+    for j in range(rows):
+        if need_all(j):
+            finish_row(j)
 
     for tile in range(rows + 1):
         for step in range(1, parts):
@@ -384,26 +415,13 @@
     assert 0 < tail and rows * tail == LANES and rows >= REACH
     modes2 = filt.shape[2]
     modes = modes2 // 2
-    bases = filt.shape[0]
-    width = rows + 2 * REACH
+    bases, width = filt.shape[0], rows + 2 * REACH
+    assert filt.shape[1] <= 256
     analysis, synth = fourier_tables(parts * lon, modes)
     ana = np.ascontiguousarray(
         analysis.reshape(parts, lon, modes2).transpose(0, 2, 1)
     ).astype(ml_dtypes.bfloat16)
     syn = synth.reshape(parts, lon, modes2).astype(ml_dtypes.bfloat16)
-    start_lat = lax.axis_index("polar") * rows
-    start_chan = lax.axis_index("azimuth") * chan_part
-    pad = ((0, 0), (REACH, REACH), (0, 0))
-    fsel = lax.dynamic_slice_in_dim(jnp.pad(filt, pad), start_lat, width, 1)
-    fsel = fsel.reshape(bases * width, modes2)
-    fsel = jnp.concatenate([fsel, fsel], axis=0)
-    goal = lax.dynamic_slice_in_dim(jnp.pad(offsets.T, pad[:2]), start_lat, width, 1) - start_lat
-    goal = goal.reshape(bases * width)
-    goal = jnp.broadcast_to(jnp.concatenate([goal, goal])[:, None], (2 * bases * width, LANES))
-    weights = lax.dynamic_slice_in_dim(basis_weight, start_chan, chan_part, 1)
-    wexp = jnp.concatenate([weights[:, :LANES]] + [weights[:, LANES:]] * rows, axis=1)
-    wexp = jnp.broadcast_to(wexp[None, :, None, :], (2, bases, width, 2 * LANES))
-    wexp = wexp.reshape(2 * bases * width, 2 * LANES)
     tiles = rows + 1
     vmem = pl.BlockSpec(memory_space=pltpu.VMEM)
     dma = pltpu.SemaphoreType.DMA
@@ -422,6 +440,7 @@
             pltpu.VMEM((width, modes2, LANES), BF16),
             pltpu.VMEM((3, modes2, LANES), BF16),
             pltpu.VMEM((tiles * reach2, modes2, LANES), F32),
+            pltpu.VMEM((modes2, 2 * bases * width), BF16),
             pltpu.VMEM((modes2, LANES), BF16),
             pltpu.VMEM((parts, tiles, lon, LANES), BF16),
             pltpu.VMEM((parts, tiles, lon, LANES), BF16),
@@ -435,8 +454,8 @@
         compiler_params=pltpu.CompilerParams(
             collective_id=0, has_side_effects=True, vmem_limit_bytes=56 * 1024 * 1024
         ),
-    )(conv_out, grad_out, w_in, b_in[None, :], w_out, wexp, goal, fsel, jnp.asarray(ana),
-      jnp.asarray(syn))
+    )(conv_out, grad_out, w_in, b_in, w_out, basis_weight, filt, offsets,
+      jnp.asarray(ana), jnp.asarray(syn))
     return (grad_out.astype(F32) + returned.astype(F32)).astype(BF16)
 
 

time: 58.8 us -> 45.5 us (0.77)
  Pallas kernels: 47.8 us -> 39.3 us
  local copies, waits for them, and re-layouts: 7.61 us -> 4.67 us
  other arithmetic: 2.96 us -> 1.36 us
    pallas_call x1, Pallas kernels: 47.8 us -> 39.3 us  [on_device(): pl.pallas_call(functools.partial(kernel, parts, bands), out_shape=jax.Sha...]
    broadcast_in_dim x3 -> x0, local copies, waits for them, and re-layouts: 2.14 us -> none  [the longest x1 1.37 us: on_device(): b_in[None, :]]
    unnamed x8 -> x4, local copies, waits for them, and re-layouts: 2.13 us -> 3.39 us
    dynamic_slice x2 -> x0, local copies, waits for them, and re-layouts: 1.07 us -> none  [the longest x1 0.99 us: on_device(): fsel = lax.dynamic_slice_in_dim(jnp.pad(filt, pad), start_lat, width, 1)]
    concatenate x3 -> x0, other arithmetic: 0.88 us -> none  [the longest x1 0.73 us: on_device(): fsel = jnp.concatenate([fsel, fsel], axis=0)]
    reshape x3 -> x0, local copies, waits for them, and re-layouts: 0.83 us -> none  [the longest x1 0.7 us: on_device(): wexp = wexp.reshape(2 * bases * width, 2 * LANES)]
    sub x1 -> x0, other arithmetic: 0.71 us -> none  [on_device(): lax.dynamic_slice_in_dim(jnp.pad(offsets.T, pad[:2]), start_lat, width, 1)]
where the time goes in v1:
time: 45.5 us; the launch traced here: 45.4 us
  Pallas kernels  39.3 us (86%)
  local copies, waits for them, and re-layouts  4.67 us (10%)
  other arithmetic  1.36 us (3%)
    pallas_call x1, Pallas kernels, on_device(): pl.pallas_call(functools.partial(kernel, parts, bands), out_shape=jax.Sha...  39.3 us
    unnamed x4, local copies, waits for them, and re-layouts  3.39 us
    convert_element_type x1, other arithmetic, on_device(): return (grad_out.astype(F32) + returned.astype(F32)).astype(BF16)  1.36 us
    convert_element_type x1, local copies, waits for them, and re-layouts, on_device(): return (grad_out.astype(F32) + returned.astype(F32)).astype(BF16)  1.28 us

profile of v1, /device:TPU:1, one launch (start us, length us, event | category | flops | bytes accessed | tf_op | source)
XLA Modules:
  0.0 45.4 jit_solution(17165927096173040425)
XLA Ops:
  0.0 0.0 copy-start
  0.0 2.3 %copy.12.conv = bf16[4,180,640]{2,1,0:T(8,128)(2,1)} copy(bf16[4,180,640]{2,0,1:T(4,128)(2,1)} %param.10) | data formatting | bytes 1843200 | tf_op args[0]
  2.3 0.0 copy-done
  2.3 1.1 %copy.11.grad = bf16[4,180,640]{2,1,0:T(8,128)(2,1)} copy(bf16[4,180,640]{2,0,1:T(4,128)(2,1)S(1)} %copy-done) | data formatting | bytes 1843200 | tf_op args[1]
  3.4 39.3 %shard_map.100 = bf16[4,180,640]{2,1,0:T(8,128)(2,1)} custom-call(bf16[4,180,640]{2,1,0:T(8,128)(2,1)} %copy.12.conv, bf16[4,180,640]{2,1,0:T(8,128)(2,1)} %copy.11.grad, bf16[640,1280]{1,0:T(8,128)(2,1)} %w_in.1, f32[1280]{0:T(1024)} %b_in.1, bf16[1280,640]{1,0:T(8,128)(2,1)} %w_out.1, f32[9,640]{1,0:T(8,128)} %weight.1, bf16[9,16,640]{2,1,0:T(8,128)(2,1)} %filt.1, ...), custom_call_target="tpu_custom_call" | custom-call | tf_op jit(solution)/shard_map/pallas_call | solution.py:429
  42.7 1.4 %add_convert_fusion = bf16[4,180,640]{2,1,0:T(8,128)(2,1)S(1)} fusion(bf16[4,180,640]{2,1,0:T(8,128)(2,1)} %shard_map.100, bf16[4,180,640]{2,0,1:T(4,128)(2,1)S(1)} %copy-done), kind=kLoop, calls=%fused_computation | loop fusion | flops 1843200 | bytes 2764800 | tf_op jit(solution)/shard_map/convert_element_type | solution.py:459
  44.1 1.3 %copy.14 = bf16[4,180,640]{2,0,1:T(4,128)(2,1)} copy(bf16[4,180,640]{2,1,0:T(8,128)(2,1)S(1)} %add_convert_fusion) | data formatting | bytes 1843200 | tf_op jit(solution)/shard_map/convert_element_type | solution.py:459
Async XLA Ops:
  0.0 2.3 %copy-start = (bf16[4,180,640]{2,0,1:T(4,128)(2,1)S(1)}, bf16[4,180,640]{2,0,1:T(4,128)(2,1)}, u32[]{:S(2)}) copy-start(bf16[4,180,640]{2,0,1:T(4,128)(2,1)} %param.11) | copy-start | bytes 2764804

commit v2 on v1

--- a/solution.py
+++ b/solution.py
@@ -46,10 +46,10 @@
 
 
 def kernel(
-    parts, bands, conv, grad, w_in, b_in, w_out, weight, filt, offsets, ana, syn,
+    parts, bands, conv_at, grad_at, w_in_at, b_in, w_out_at, weight, filt, offsets, ana_at, syn_at,
     out,
-    w_perm, slope, tails, send, recv, spec, spec_tail, gain, flipped, outspec, ret_send, ret_recv,
-    a_send, a_recv, z_send, z_recv, r_send, r_recv,
+    conv_n, grad_n, conv, grad, w_in, w_out, ana, syn, w_perm, slope, tails, send, recv, spec, spec_tail, gain, flipped, outspec, ret_send, ret_recv,
+    a_send, a_recv, z_send, z_recv, r_send, r_recv, loads,
 ):
     rows, lon, channels = conv.shape
     hidden = w_in.shape[1]
@@ -78,14 +78,22 @@
     def _():
         pl.semaphore_signal(barrier, inc=1, device_id={"polar": band + 1}, device_id_type=MESH)
 
+    pairs = [(conv_at, conv_n), (w_in_at, w_in), (grad_at, grad_n), (w_out_at, w_out)]
     for part in range(parts):
-        w_perm[part * LANES : (part + 1) * LANES, :] = w_in[
-            part * chan_part : part * chan_part + LANES, :
-        ]
-        w_perm[parts * LANES + part * tail : parts * LANES + (part + 1) * tail, :] = w_in[
-            part * chan_part + LANES : (part + 1) * chan_part, :
-        ]
-
+        split = part * chan_part + LANES
+        pairs.append((w_in_at.at[part * chan_part : split], w_perm.at[part * LANES : (part + 1) * LANES]))
+        begin = parts * LANES + part * tail
+        pairs.append((w_in_at.at[split : split + tail], w_perm.at[begin : begin + tail]))
+    pairs += [(ana_at, ana), (syn_at, syn)]
+    copies = [pltpu.make_async_copy(src, dst, loads.at[n]) for n, (src, dst) in enumerate(pairs)]
+    for copy in copies:
+        copy.start()
+    copies[0].wait()
+    conv[...] = jnp.transpose(conv_n[...], (1, 0, 2))
+    copies[2].wait()
+    grad[...] = jnp.transpose(grad_n[...], (1, 0, 2))
+    for copy in [copies[1]] + copies[3:-1]:
+        copy.wait()
     neighbours = jnp.where(has_low, 1, 0) + jnp.where(has_high, 1, 0)
     pl.semaphore_wait(barrier, parts - 1 + neighbours)
 
@@ -110,8 +118,7 @@
 
     piece = 2 * LANES
 
-    def mlp_row(it, carry):
-        row = row_order(it)
+    def mlp_row(row):
         for at in range(0, hidden, piece):
             pre = dot(conv[row], w_in[:, at : at + piece]) + b_in[at : at + piece][None, :]
             back = dot_nt(grad[row], w_out[at : at + piece, :])
@@ -123,16 +130,6 @@
         recv[row, me] = send[me, row]
         for step in range(1, parts):
             out_copy(step, row).start()
-        return carry
-
-    lax.fori_loop(0, rows, mlp_row, 0)
-    for part in range(parts):
-        send[part, rows] = jnp.concatenate(
-            [tails[row][:, part * tail : (part + 1) * tail] for row in range(rows)], axis=1
-        )
-    recv[rows, me] = send[me, rows]
-    for step in range(1, parts):
-        out_copy(step, rows).start()
 
     @pl.when(jnp.logical_not(has_low))
     def _():
@@ -145,7 +142,7 @@
         spec_tail[2] = jnp.zeros((modes2, LANES), BF16)
 
     def up_copy(row):
-        if row == rows:
+        if isinstance(row, int) and row == rows:
             src, dst = spec_tail.at[1], spec_tail.at[0]
         else:
             src, dst = spec.at[REACH + row], spec.at[REACH + row - rows]
@@ -155,7 +152,7 @@
         )
 
     def down_copy(row):
-        if row == rows:
+        if isinstance(row, int) and row == rows:
             src, dst = spec_tail.at[1], spec_tail.at[2]
         else:
             src, dst = spec.at[REACH + row], spec.at[REACH + row + rows]
@@ -182,22 +179,44 @@
             total = total + dot(ana[src], recv[tile, src])
         return total.astype(BF16)
 
-    order = [it * (rows - 1) % rows for it in range(rows)]
-    done = []
-    ups = list(range(rows - 1, rows - REACH, -1))
-    downs = list(range(REACH - 1))
-    for row in order:
-        spec[REACH + row] = analyze(row)
-        done.append(row)
-        while ups and ups[0] in done:
-            start_up(ups.pop(0))
-        while downs and downs[0] in done:
-            start_down(downs.pop(0))
+    delay = 2
+
+    def advance(it, carry):
+        @pl.when(it < rows)
+        def _():
+            mlp_row(row_order(it))
+
+        @pl.when(it == rows - 1)
+        def _():
+            for part in range(parts):
+                send[part, rows] = jnp.concatenate(
+                    [tails[row][:, part * tail : (part + 1) * tail] for row in range(rows)], axis=1
+                )
+            recv[rows, me] = send[me, rows]
+            for step in range(1, parts):
+                out_copy(step, rows).start()
+
+        @pl.when(it >= delay)
+        def _():
+            row = row_order(it - delay)
+            spec[REACH + row] = analyze(row)
+
+            @pl.when(has_high & (row >= rows - REACH))
+            def _():
+                up_copy(row).start()
+
+            @pl.when(has_low & (row == 0))
+            def _():
+                down_copy(row).start()
+
+        return carry
+
+    lax.fori_loop(0, rows + delay, advance, 0)
+    for row in range(1, REACH):
+        start_down(row)
     spec_tail[1] = analyze(rows)
     start_up(rows)
     start_down(rows)
-    start_up(rows - REACH)
-    start_down(REACH - 1)
 
     half = bases * width
     lines = 2 * half
@@ -330,6 +349,7 @@
 
         lax.fori_loop(0, modes // chunk, one, 0)
 
+    copies[-1].wait()
     low_left = list(range(rows - REACH, rows))
     high_left = list(range(REACH))
 
@@ -360,9 +380,8 @@
         filter_main(j)
         finish(j)
 
-    for j in range(rows):
-        if not need_all(j):
-            finish_row(j)
+    for j in sorted(range(rows), key=need_all):
+        finish_row(j)
 
     @pl.when(has_low)
     def _():
@@ -374,9 +393,6 @@
 
     filter_tail()
     finish(rows)
-    for j in range(rows):
-        if need_all(j):
-            finish_row(j)
 
     for tile in range(rows + 1):
         for step in range(1, parts):
@@ -401,7 +417,8 @@
         for src in range(parts):
             pieces.append(ret_recv[src, row])
             pieces.append(ret_recv[src, rows][:, row * tail : (row + 1) * tail])
-        out[row] = jnp.concatenate(pieces, axis=1)
+        conv[row] = jnp.concatenate(pieces, axis=1)
+    out[...] = jnp.transpose(conv[...], (1, 0, 2))
     for tile in range(rows + 1):
         for step in range(1, parts):
             back_copy(step, tile).wait_send()
@@ -424,14 +441,23 @@
     syn = synth.reshape(parts, lon, modes2).astype(ml_dtypes.bfloat16)
     tiles = rows + 1
     vmem = pl.BlockSpec(memory_space=pltpu.VMEM)
+    hbm = pl.BlockSpec(memory_space=pl.ANY)
     dma = pltpu.SemaphoreType.DMA
     reach2 = 2 * REACH + 1
     returned = pl.pallas_call(
         functools.partial(kernel, parts, bands),
-        out_shape=jax.ShapeDtypeStruct((rows, lon, channels), BF16),
-        in_specs=[vmem] * 10,
+        out_shape=jax.ShapeDtypeStruct((lon, rows, channels), BF16),
+        in_specs=[hbm, hbm, hbm, vmem, hbm, vmem, vmem, vmem, hbm, hbm],
         out_specs=vmem,
         scratch_shapes=[
+            pltpu.VMEM((lon, rows, channels), BF16),
+            pltpu.VMEM((lon, rows, channels), BF16),
+            pltpu.VMEM((rows, lon, channels), BF16),
+            pltpu.VMEM((rows, lon, channels), BF16),
+            pltpu.VMEM(w_in.shape, BF16),
+            pltpu.VMEM(w_out.shape, BF16),
+            pltpu.VMEM(ana.shape, BF16),
+            pltpu.VMEM(syn.shape, BF16),
             pltpu.VMEM((channels, hidden), BF16),
             pltpu.VMEM((lon, hidden), BF16),
             pltpu.VMEM((rows, lon, parts * tail), BF16),
@@ -450,13 +476,14 @@
             dma((2, tiles)),
             dma((parts, tiles)),
             dma((parts, tiles)),
+            dma((6 + 2 * parts,)),
         ],
         compiler_params=pltpu.CompilerParams(
             collective_id=0, has_side_effects=True, vmem_limit_bytes=56 * 1024 * 1024
         ),
-    )(conv_out, grad_out, w_in, b_in, w_out, basis_weight, filt, offsets,
+    )(jnp.transpose(conv_out, (1, 0, 2)), jnp.transpose(grad_out, (1, 0, 2)), w_in, b_in, w_out, basis_weight, filt, offsets,
       jnp.asarray(ana), jnp.asarray(syn))
-    return (grad_out.astype(F32) + returned.astype(F32)).astype(BF16)
+    return (grad_out.astype(F32) + jnp.transpose(returned, (1, 0, 2)).astype(F32)).astype(BF16)
 
 
 def solution(mesh):

time: 45.5 us -> 41.5 us (0.912)
  local copies, waits for them, and re-layouts: 4.67 us -> 0.01 us
  other arithmetic: 1.36 us -> 2.58 us
  Pallas kernels: 39.3 us -> 38.8 us
    unnamed x4 -> x2, local copies, waits for them, and re-layouts: 3.39 us -> 0.01 us
    convert_element_type x1 -> x0, local copies, waits for them, and re-layouts: 1.28 us -> none  [on_device(): return (grad_out.astype(F32) + returned.astype(F32)).astype(BF16)]
    convert_element_type x1, other arithmetic: 1.36 us -> 2.58 us  [on_device(): (grad_out.astype(F32) + jnp.transpose(returned, (1, 0, 2)).astype(F32)).a...]
    pallas_call x1, Pallas kernels: 39.3 us -> 38.8 us  [on_device(): pl.pallas_call(functools.partial(kernel, parts, bands), out_shape=jax.Sha...]
where the time goes in v2:
time: 41.5 us; the launch traced here: 41.4 us
  Pallas kernels  38.8 us (93%)
  other arithmetic  2.58 us (6%)
    pallas_call x1, Pallas kernels, on_device(): pl.pallas_call(functools.partial(kernel, parts, bands), out_shape=jax.Sha...  38.8 us
    convert_element_type x1, other arithmetic, on_device(): (grad_out.astype(F32) + jnp.transpose(returned, (1, 0, 2)).astype(F32)).a...  2.58 us

profile of v2, /device:TPU:1, one launch (start us, length us, event | category | flops | bytes accessed | tf_op | source)
XLA Modules:
  0.0 41.4 jit_solution(7119470440037740111)
XLA Ops:
  0.0 0.0 copy-start
  0.0 38.8 %shard_map.100 = bf16[180,4,640]{2,1,0:T(4,128)(2,1)} custom-call(bf16[180,4,640]{2,1,0:T(4,128)(2,1)} %bitcast.7, bf16[180,4,640]{2,1,0:T(4,128)(2,1)} %bitcast.6, bf16[640,1280]{1,0:T(8,128)(2,1)} %w_in_at.1, f32[1280]{0:T(1024)} %b_in.1, bf16[1280,640]{1,0:T(8,128)(2,1)} %w_out_at.1, f32[9,640]{1,0:T(8,128)} %weight.1, bf16[9,16,640]{2,1,0:T(8,128)(2,1)} %filt.1, ...), custom_call_target="tpu_custom_call" | custom-call | tf_op jit(solution)/shard_map/pallas_call | solution.py:447
  38.8 0.0 copy-done
  38.8 2.6 %fusion = bf16[4,180,640]{2,0,1:T(4,128)(2,1)} fusion(bf16[180,4,640]{2,1,0:T(4,128)(2,1)} %shard_map.100, bf16[4,180,640]{2,0,1:T(4,128)(2,1)S(1)} %copy-done), kind=kLoop, calls=%fused_computation.1 | loop fusion | flops 1843200 | bytes 2764800 | tf_op jit(solution)/shard_map/convert_element_type | solution.py:486
Async XLA Ops:
  0.0 38.8 %copy-start = (bf16[4,180,640]{2,0,1:T(4,128)(2,1)S(1)}, bf16[4,180,640]{2,0,1:T(4,128)(2,1)}, u32[]{:S(2)}) copy-start(bf16[4,180,640]{2,0,1:T(4,128)(2,1)} %param.11) | copy-start | bytes 2764804

commit v3 on v2

--- a/solution.py
+++ b/solution.py
@@ -417,7 +417,8 @@
         for src in range(parts):
             pieces.append(ret_recv[src, row])
             pieces.append(ret_recv[src, rows][:, row * tail : (row + 1) * tail])
-        conv[row] = jnp.concatenate(pieces, axis=1)
+        total = grad[row].astype(F32) + jnp.concatenate(pieces, axis=1).astype(F32)
+        conv[row] = total.astype(BF16)
     out[...] = jnp.transpose(conv[...], (1, 0, 2))
     for tile in range(rows + 1):
         for step in range(1, parts):
@@ -444,7 +445,7 @@
     hbm = pl.BlockSpec(memory_space=pl.ANY)
     dma = pltpu.SemaphoreType.DMA
     reach2 = 2 * REACH + 1
-    returned = pl.pallas_call(
+    result = pl.pallas_call(
         functools.partial(kernel, parts, bands),
         out_shape=jax.ShapeDtypeStruct((lon, rows, channels), BF16),
         in_specs=[hbm, hbm, hbm, vmem, hbm, vmem, vmem, vmem, hbm, hbm],
@@ -483,7 +484,7 @@
         ),
     )(jnp.transpose(conv_out, (1, 0, 2)), jnp.transpose(grad_out, (1, 0, 2)), w_in, b_in, w_out, basis_weight, filt, offsets,
       jnp.asarray(ana), jnp.asarray(syn))
-    return (grad_out.astype(F32) + jnp.transpose(returned, (1, 0, 2)).astype(F32)).astype(BF16)
+    return jnp.transpose(result, (1, 0, 2))
 
 
 def solution(mesh):

time: 41.5 us -> 41.3 us (level)
  other arithmetic: 2.58 us -> 0 us
  local copies, waits for them, and re-layouts: 0.01 us -> 2.42 us
    convert_element_type x1 -> x0, other arithmetic: 2.58 us -> none  [on_device(): (grad_out.astype(F32) + jnp.transpose(returned, (1, 0, 2)).astype(F32)).a...]
    unnamed x2 -> x1, local copies, waits for them, and re-layouts: 0.01 us -> 2.42 us
where the time goes in v3:
time: 41.3 us; the launch traced here: 41.2 us
  Pallas kernels  38.7 us (94%)
  local copies, waits for them, and re-layouts  2.42 us (6%)
    pallas_call x1, Pallas kernels, on_device(): pl.pallas_call(functools.partial(kernel, parts, bands), out_shape=jax.Sha...  38.7 us
    unnamed x1, local copies, waits for them, and re-layouts  2.42 us

profile of v3, /device:TPU:1, one launch (start us, length us, event | category | flops | bytes accessed | tf_op | source)
XLA Modules:
  0.0 41.2 jit_solution(2275901625317550297)
XLA Ops:
  0.0 38.7 %shard_map.100 = bf16[180,4,640]{2,1,0:T(4,128)(2,1)} custom-call(bf16[180,4,640]{2,1,0:T(4,128)(2,1)} %bitcast.4, bf16[180,4,640]{2,1,0:T(4,128)(2,1)} %bitcast.5, bf16[640,1280]{1,0:T(8,128)(2,1)} %w_in_at.1, f32[1280]{0:T(1024)} %b_in.1, bf16[1280,640]{1,0:T(8,128)(2,1)} %w_out_at.1, f32[9,640]{1,0:T(8,128)} %weight.1, bf16[9,16,640]{2,1,0:T(8,128)(2,1)} %filt.1, ...), custom_call_target="tpu_custom_call" | custom-call | tf_op jit(solution)/shard_map/pallas_call | solution.py:448
  38.7 2.4 %copy.12 = bf16[4,180,640]{2,0,1:T(4,128)(2,1)} copy(bf16[4,180,640]{2,0,1:T(4,128)(2,1)} %bitcast.3) | data formatting | bytes 1843200
